TPU v7x, 256 devices: a whole 4x4x8 slice. The times are simulated.
256 devices in a mesh: dp: 16 (over z_hi, y), fsdp: 16 (over x, z_lo, core).
Axes of the slice: x: 4, y: 4, z: 8 (z_hi: 4, z_lo: 2; z = z_hi * 2 + z_lo), core: 2. Of those that a mesh axis runs over, the one named last changes fastest.
Arguments:
- features: bfloat16 [49152, 8192], P(('dp', 'fsdp')), may hold values from -6 to 6
- grad_out: bfloat16 [49152, 8192], P(('dp', 'fsdp')), may hold values from -6 to 6
- weight_tiles: bfloat16 [256, 128, 128], P('fsdp'), may hold values from -0.25 to 0.25
- tile_row: int32 [256], replicated, may hold values from 0 to 63, as said below
- tile_column: int32 [256], replicated, may hold values from 0 to 63, as said below
Outputs:
- grad_features: bfloat16 [49152, 8192], P(('dp', 'fsdp'))
- tile_update: float32 [256, 128, 128], P('fsdp')
Inputs may be any that keep to these rules, and one draw needn't show every extreme that they name: `tile_row`: every tile-row holds exactly 4 stored tiles; the tile-columns of tile-row i are i XOR s for the four values s in (0, 2^a, 2^b, 2^a + 2^b), with two distinct bits a, b drawn per run; the stored order is a random permutation of the pattern. Every tile-column holds exactly 4 stored tiles; no (tile_row, tile_column) pair appears twice.
All inputs are finite; a program needn't handle non-finite values.
Results may differ from a plain program's by a relative error of at most 0.0034.
Values may be sent and summed in bfloat16 or wider, within the bound.
No kernel may reach another device: no remote copies, remote signals or barrier semaphores. Data moves between devices by JAX's collectives and lax.ppermute only.
A program may use at most 128 MiB of HBM per device.

v0:
```python
import math
import jax
import jax.numpy as jnp
from jax import lax
from jax.sharding import PartitionSpec as P


def gelu_slope(value):
    root_term = math.sqrt(2.0 / math.pi)
    inner = root_term * (value + 0.044715 * value * value * value)
    hyper = jnp.tanh(inner)
    return 0.5 * (1.0 + hyper) + 0.5 * value * (1.0 - hyper * hyper) * root_term * (
        1.0 + 3.0 * 0.044715 * value * value
    )


def on_device(features, grad_out, weight_tiles, tile_row, tile_column):
    rows_here = features.shape[0]
    side = weight_tiles.shape[1]
    nblocks = features.shape[1] // side
    total_tiles = tile_row.shape[0]
    per_block = total_tiles // nblocks
    feature_blocks = features.reshape(rows_here, nblocks, side)
    grad_blocks = grad_out.reshape(rows_here, nblocks, side)
    order_rows = jnp.argsort(tile_row, stable=True)
    order_columns = jnp.argsort(tile_column, stable=True)
    columns_by_row = tile_column[order_rows].reshape(nblocks, per_block)
    rows_by_column = tile_row[order_columns].reshape(nblocks, per_block)
    whole = lax.all_gather(weight_tiles, "fsdp", axis=0, tiled=True)
    tiles_by_row = whole[order_rows].reshape(nblocks, per_block, side, side)
    taken = feature_blocks[:, columns_by_row]
    preact = jnp.einsum("rnkc,nkcd->rnd", taken, tiles_by_row, preferred_element_type=jnp.float32)
    slope_grad = (grad_blocks.astype(jnp.float32) * gelu_slope(preact)).astype(jnp.bfloat16)
    tiles_by_column = whole[order_columns].reshape(nblocks, per_block, side, side)
    slopes_taken = slope_grad[:, rows_by_column]
    returned = jnp.einsum(
        "rnkd,nkcd->rnc", slopes_taken, tiles_by_column, preferred_element_type=jnp.float32
    )
    grad_features = (
        (grad_blocks.astype(jnp.float32) + returned)
        .astype(jnp.bfloat16)
        .reshape(rows_here, nblocks * side)
    )
    tile_ids = jnp.arange(
        total_tiles // lax.axis_size("fsdp") * lax.axis_size("fsdp"), dtype=jnp.int32
    )
    columns = tile_column[tile_ids]
    row_ids = tile_row[tile_ids]
    picked = jnp.take(feature_blocks, columns, axis=1)
    slopes = jnp.take(slope_grad, row_ids, axis=1)
    summed = lax.psum_scatter(
        jnp.einsum("rnc,rnd->ncd", picked, slopes, preferred_element_type=jnp.float32),
        "fsdp",
        scatter_dimension=0,
        tiled=True,
    )
    weight_grad = lax.psum(summed, "dp")
    tile_update = weight_grad * lax.rsqrt(
        jnp.mean(weight_grad * weight_grad, axis=(1, 2), keepdims=True) + 1e-06
    )
    return (grad_features, tile_update)


def solution(mesh):
    return jax.shard_map(
        on_device,
        mesh=mesh,
        in_specs=(
            P(("dp", "fsdp"), None),
            P(("dp", "fsdp"), None),
            P("fsdp", None, None),
            P(),
            P(),
        ),
        out_specs=(P(("dp", "fsdp"), None), P("fsdp", None, None)),
        check_vma=False,
    )
```

profile of v0, /device:TPU:8, one launch (start us, length us, event | category | flops | bytes accessed | tf_op | source)
XLA Modules:
  0.0 482.4 jit_solution(4299826176216152528)
XLA Ops:
  7.2 0.0 all-gather.2.cloned.1.call-start
  7.2 0.7 all-gather.2.cloned.1.call-update
  7.9 0.0 reduce-scatter.2.cloned.1.call-start
  8.0 4.0 sort.32
  12.0 2.0 gather_fusion.7
  13.9 2.0 gather_fusion.6
  16.0 2.0 gather_fusion.2
  17.9 0.1 reshape.97
  18.1 0.1 reshape.143
  18.2 2.6 copy_bitcast_fusion.1
  20.7 12.8 %gather_fusion.3 = bf16[256,192,128]{2,1,0:T(8,128)(2,1)} fusion(bf16[192,64,128]{2,0,1:T(8,128)(2,1)} %copy_bitcast_fusion.1, s32[1024]{0:T(1024)S(1)} %pad_clamp_fusion.4), kind=kCustom, calls=%fused_computation.5 | custom fusion | bytes 25166848 | tf_op jit(solution)/shard_map/gather | solution.py:31
  33.6 10.8 %gather_fusion.8 = bf16[256,192,128]{2,1,0:T(8,128)(2,1)} fusion(bf16[192,64,128]{2,0,1:T(8,128)(2,1)S(1)} %copy-done.4, s32[1024]{0:T(1024)S(1)} %pad_clamp_fusion.1), kind=kCustom, calls=%fused_computation.clone | custom fusion | bytes 25166848 | tf_op jit(solution)/shard_map/jit(_take)/gather | solution.py:49
  44.4 23.1 %all-gather.2.cloned.1.call-done = bf16[256,128,128]{2,1,0:T(8,128)(2,1)} async-done(((bf16[16,128,128]{2,1,0:T(8,128)(2,1)}), bf16[256,128,128]{2,1,0:T(8,128)(2,1)}) %all-gather.2.cloned.1.call-update) | async-done | bytes 8388624 | tf_op jit(solution)/shard_map/all_gather | solution.py:29
  67.5 12.1 %gather_fusion.1 = bf16[256,128,128]{2,1,0:T(8,128)(2,1)} fusion(bf16[256,128,128]{2,1,0:T(8,128)(2,1)} %all-gather.2.cloned.1.call-done, s32[1024]{0:T(1024)S(1)} %pad_clamp_fusion.5), kind=kCustom, calls=%fused_computation.3 | custom fusion | bytes 16778240 | tf_op jit(solution)/shard_map/gather | solution.py:30
  79.6 11.0 %fusion.13 = bf16[192,64,128]{2,0,1:T(8,128)(2,1)S(1)} fusion(bf16[192,64,4,128]{3,0,2,1:T(8,128)(2,1)} %bitcast.65, bf16[64,4,128,128]{3,2,1,0:T(8,128)(2,1)} %bitcast.68, bf16[192,8192]{1,0:T(8,128)(2,1)} %param.8), kind=kOutput, calls=%fused_computation.25 | convolution fusion | flops 1642070016 | bytes 27262976 | tf_op jit(solution)/shard_map/rnkc,nkcd->rnd/dot_general | solution.py:32
  90.6 10.7 %gather_fusion.9 = bf16[256,192,128]{2,1,0:T(8,128)(2,1)} fusion(bf16[192,64,128]{2,0,1:T(8,128)(2,1)S(1)} %fusion.13, s32[1024]{0:T(1024)S(1)} %pad_clamp_fusion), kind=kCustom, calls=%fused_computation.1.clone | custom fusion | bytes 25166848 | tf_op jit(solution)/shard_map/jit(_take)/gather | solution.py:50
  101.4 14.6 %fusion = f32[256,128,128]{2,1,0:T(8,128)} fusion(bf16[256,192,128]{2,1,0:T(8,128)(2,1)} %gather_fusion.9, bf16[256,192,128]{2,1,0:T(8,128)(2,1)} %gather_fusion.8, pred[256]{0:T(512)(128)(4,1)S(1)} %get-tuple-element.7, pred[256]{0:T(512)(128)(4,1)S(1)} %get-tuple-element.8), kind=kOutput, calls=%fused_computation.10 | convolution fusion | flops 1623195648 | bytes 41943552 | tf_op jit(solution)/shard_map/rnc,rnd->ncd/dot_general | solution.py:52
  116.0 0.0 reduce-scatter.2.cloned.1.call-update
  116.0 0.0 all-reduce.2.cloned.1.call-start
  116.1 0.6 copy-done.2
  116.7 3.2 sort.31
  119.9 2.2 gather_fusion.4
  122.1 0.1 reshape.98
  122.2 0.1 reshape.159
  122.3 12.4 %gather_fusion.5 = bf16[256,192,128]{2,1,0:T(8,128)(2,1)} fusion(bf16[192,64,128]{2,0,1:T(8,128)(2,1)} %copy-done.5, s32[1024]{0:T(1024)S(1)} %pad_clamp_fusion.3), kind=kCustom, calls=%fused_computation.7 | custom fusion | bytes 25166848 | tf_op jit(solution)/shard_map/gather | solution.py:35
  134.7 12.2 %gather_fusion = bf16[256,128,128]{2,1,0:T(8,128)(2,1)} fusion(bf16[256,128,128]{2,1,0:T(8,128)(2,1)} %all-gather.2.cloned.1.call-done, s32[1024]{0:T(1024)S(1)} %pad_clamp_fusion.6), kind=kCustom, calls=%fused_computation.2 | custom fusion | bytes 16778240 | tf_op jit(solution)/shard_map/gather | solution.py:34
  146.9 155.1 %reduce-scatter.2.cloned.1.call-done = f32[16,128,128]{2,1,0:T(8,128)} async-done(((f32[256,128,128]{2,1,0:T(8,128)}), f32[16,128,128]{2,1,0:T(8,128)}) %reduce-scatter.2.cloned.1.call-update) | async-done | bytes 1048592 | tf_op jit(solution)/shard_map/reduce_scatter | solution.py:51
  302.0 12.5 %fusion.18 = bf16[64,24,8,128]{3,2,1,0:T(8,128)(2,1)} fusion(bf16[64,4,128,128]{3,2,1,0:T(8,128)(2,1)} %bitcast.67, bf16[192,64,4,128]{3,0,2,1:T(8,128)(2,1)} %bitcast.66, bf16[192,8192]{1,0:T(8,128)(2,1)} %param.8), kind=kOutput, calls=%fused_computation.33 | convolution fusion | flops 1615331328 | bytes 27262976 | tf_op jit(solution)/shard_map/rnkd,nkcd->rnc/dot_general | solution.py:36
  314.5 4.4 copy.32
  319.0 153.1 %all-reduce.2.cloned.1.call-done = f32[16,128,128]{2,1,0:T(8,128)} async-done(((f32[16,128,128]{2,1,0:T(8,128)}), f32[16,128,128]{2,1,0:T(8,128)}) %all-reduce.2.cloned.1.call-update) | async-done | bytes 1048592 | tf_op jit(solution)/shard_map/psum | solution.py:57
  472.1 1.4 multiply_reduce_fusion
  473.5 2.3 broadcast_multiply_fusion
  (30 shorter events, 0.2 us)
Async XLA Ops:
  7.2 11.0 %copy-start = (bf16[192,8192]{1,0:T(8,128)(2,1)S(1)}, bf16[192,8192]{1,0:T(8,128)(2,1)}, u32[]{:S(2)}) copy-start(bf16[192,8192]{1,0:T(8,128)(2,1)} %param.7) | copy-start | bytes 9437188
  7.2 60.3 %all-gather.2.cloned.1.call-start = ((), (), s32[]{:S(2)}) async-start(), calls=%async_computation.1 | async-start | bytes 8912896 | tf_op jit(solution)/shard_map/all_gather | solution.py:29
  7.9 294.0 %reduce-scatter.2.cloned.1.call-start = ((), (), s32[]{:S(2)}) async-start(), calls=%async_computation.2 | async-start | bytes 17825792 | tf_op jit(solution)/shard_map/reduce_scatter | solution.py:51
  20.7 12.9 %copy-start.4 = (bf16[192,64,128]{2,0,1:T(8,128)(2,1)S(1)}, bf16[192,64,128]{2,0,1:T(8,128)(2,1)}, u32[]{:S(2)}) copy-start(bf16[192,64,128]{2,0,1:T(8,128)(2,1)} %copy_bitcast_fusion.1) | copy-start | bytes 9437188
  90.6 10.7 %copy-start.5 = (bf16[192,64,128]{2,0,1:T(8,128)(2,1)}, bf16[192,64,128]{2,0,1:T(8,128)(2,1)S(1)}, u32[]{:S(2)}) copy-start(bf16[192,64,128]{2,0,1:T(8,128)(2,1)S(1)} %fusion.13) | copy-start | bytes 9437188
  116.0 0.7 copy-start.2
  116.0 3.9 copy-start.3
  116.0 356.1 %all-reduce.2.cloned.1.call-start = ((), (), s32[]{:S(2)}) async-start(), calls=%async_computation.3 | async-start | bytes 2097152 | tf_op jit(solution)/shard_map/psum | solution.py:57
  302.0 173.9 %copy-start.1 = (bf16[192,8192]{1,0:T(8,128)(2,1)S(1)}, bf16[192,8192]{1,0:T(8,128)(2,1)}, u32[]{:S(2)}) copy-start(bf16[192,8192]{1,0:T(8,128)(2,1)} %param.7) | copy-start | bytes 9437188
Sparse Core Ops, SparseCore 0:
  9.9 57.6 all-gather.1
  116.2 185.7 reduce-scatter.1
  304.6 167.4 all-reduce.1
where the time goes:
time: 483 us; the launch traced here: 482 us
  waiting for transfers between devices  332 us (69%)
  local copies, waits for them, and re-layouts  87.2 us (18%)
  matrix products  38.2 us (8%)
  between operations  13.9 us (3%)
  other arithmetic  11 us (2%)
    reduce_scatter x1, waiting for transfers between devices, on_device(): lax.psum_scatter(jnp.einsum('rnc,rnd->ncd', picked, slopes, preferred_ele...  155 us
    psum x1, waiting for transfers between devices, on_device(): weight_grad = lax.psum(summed, 'dp')  153 us
    all_gather x1, waiting for transfers between devices, on_device(): whole = lax.all_gather(weight_tiles, 'fsdp', axis=0, tiled=True)  23.1 us
    dot_general x1, matrix products, on_device(): jnp.einsum('rnc,rnd->ncd', picked, slopes, preferred_element_type=jnp.flo...  14.6 us
    gather x1, local copies, waits for them, and re-layouts, on_device(): taken = feature_blocks[:, columns_by_row]  12.8 us
    dot_general x1, matrix products, on_device(): jnp.einsum('rnkd,nkcd->rnc', slopes_taken, tiles_by_column, preferred_ele...  12.5 us
    gather x1, local copies, waits for them, and re-layouts, on_device(): slopes_taken = slope_grad[:, rows_by_column]  12.4 us
    gather x1, local copies, waits for them, and re-layouts, on_device(): whole[order_columns].reshape(nblocks, per_block, side, side)  12.2 us
  transfers between devices with their start and end apart: 3, of which 3 were waited for; matrix products, arithmetic and copies ran while one was open for 17% of the time, Pallas kernels for 0%

commit v1 on v0

--- a/solution.py
+++ b/solution.py
@@ -54,7 +54,7 @@
         scatter_dimension=0,
         tiled=True,
     )
-    weight_grad = lax.psum(summed, "dp")
+    weight_grad = jax.lax.all_gather(summed, "dp").sum(axis=0)
     tile_update = weight_grad * lax.rsqrt(
         jnp.mean(weight_grad * weight_grad, axis=(1, 2), keepdims=True) + 1e-06
     )

time: 483 us -> 525 us (1.087)
  the two profiles are of different devices: /device:TPU:8 before, /device:TPU:2 now
where the time goes in v1:
time: 525 us; the launch traced here: 524 us
  waiting for transfers between devices  369 us (70%)
  local copies, waits for them, and re-layouts  85.1 us (16%)
  matrix products  36.9 us (7%)
  other arithmetic  19.6 us (4%)
  between operations  13.9 us (3%)
    reduce_scatter x1, waiting for transfers between devices, on_device(): lax.psum_scatter(jnp.einsum('rnc,rnd->ncd', picked, slopes, preferred_ele...  184 us
    all_gather x1, waiting for transfers between devices, on_device(): weight_grad = jax.lax.all_gather(summed, 'dp').sum(axis=0)  161 us
    all_gather x1, waiting for transfers between devices, on_device(): whole = lax.all_gather(weight_tiles, 'fsdp', axis=0, tiled=True)  23 us
    dot_general x1, matrix products, on_device(): jnp.einsum('rnc,rnd->ncd', picked, slopes, preferred_element_type=jnp.flo...  14.6 us
    gather x1, local copies, waits for them, and re-layouts, on_device(): slopes_taken = slope_grad[:, rows_by_column]  12.9 us
    gather x1, local copies, waits for them, and re-layouts, on_device(): taken = feature_blocks[:, columns_by_row]  12.8 us
    gather x1, local copies, waits for them, and re-layouts, on_device(): whole[order_columns].reshape(nblocks, per_block, side, side)  12.1 us
    gather x1, local copies, waits for them, and re-layouts, on_device(): tiles_by_row = whole[order_rows].reshape(nblocks, per_block, side, side)  12.1 us
  transfers between devices with their start and end apart: 3, of which 3 were waited for; matrix products, arithmetic and copies ran while one was open for 15% of the time, Pallas kernels for 0%

profile of v1, /device:TPU:2, one launch (start us, length us, event | category | flops | bytes accessed | tf_op | source)
XLA Modules:
  0.0 524.4 jit_solution(17040093149918109024)
XLA Ops:
  7.2 0.0 all-gather.4.cloned.1.call-start
  7.2 0.7 all-gather.4.cloned.1.call-update
  7.9 0.0 reduce-scatter.2.cloned.1.call-start
  8.0 4.0 sort.32
  12.0 2.0 gather_fusion.7
  13.9 2.0 gather_fusion.6
  16.0 2.0 gather_fusion.2
  17.9 0.1 reshape.97
  18.1 0.1 reshape.143
  18.2 2.6 copy_bitcast_fusion.1
  20.7 12.8 %gather_fusion.3 = bf16[256,192,128]{2,1,0:T(8,128)(2,1)} fusion(bf16[192,64,128]{2,0,1:T(8,128)(2,1)} %copy_bitcast_fusion.1, s32[1024]{0:T(1024)S(1)} %pad_clamp_fusion.4), kind=kCustom, calls=%fused_computation.5 | custom fusion | bytes 25166848 | tf_op jit(solution)/shard_map/gather | solution.py:31
  33.6 10.8 %gather_fusion.8 = bf16[256,192,128]{2,1,0:T(8,128)(2,1)} fusion(bf16[192,64,128]{2,0,1:T(8,128)(2,1)S(1)} %copy-done.4, s32[1024]{0:T(1024)S(1)} %pad_clamp_fusion.1), kind=kCustom, calls=%fused_computation.clone | custom fusion | bytes 25166848 | tf_op jit(solution)/shard_map/jit(_take)/gather | solution.py:49
  44.4 23.0 %all-gather.4.cloned.1.call-done = bf16[256,128,128]{2,1,0:T(8,128)(2,1)} async-done(((bf16[16,128,128]{2,1,0:T(8,128)(2,1)}), bf16[256,128,128]{2,1,0:T(8,128)(2,1)}) %all-gather.4.cloned.1.call-update) | async-done | bytes 8388624 | tf_op jit(solution)/shard_map/all_gather | solution.py:29
  67.4 12.1 %gather_fusion.1 = bf16[256,128,128]{2,1,0:T(8,128)(2,1)} fusion(bf16[256,128,128]{2,1,0:T(8,128)(2,1)} %all-gather.4.cloned.1.call-done, s32[1024]{0:T(1024)S(1)} %pad_clamp_fusion.5), kind=kCustom, calls=%fused_computation.3 | custom fusion | bytes 16778240 | tf_op jit(solution)/shard_map/gather | solution.py:30
  79.5 11.0 %fusion.13 = bf16[192,64,128]{2,0,1:T(8,128)(2,1)S(1)} fusion(bf16[192,64,4,128]{3,0,2,1:T(8,128)(2,1)} %bitcast.67, bf16[64,4,128,128]{3,2,1,0:T(8,128)(2,1)} %bitcast.70, bf16[192,8192]{1,0:T(8,128)(2,1)} %param.8), kind=kOutput, calls=%fused_computation.25 | convolution fusion | flops 1642070016 | bytes 27262976 | tf_op jit(solution)/shard_map/rnkc,nkcd->rnd/dot_general | solution.py:32
  90.5 10.7 %gather_fusion.9 = bf16[256,192,128]{2,1,0:T(8,128)(2,1)} fusion(bf16[192,64,128]{2,0,1:T(8,128)(2,1)S(1)} %fusion.13, s32[1024]{0:T(1024)S(1)} %pad_clamp_fusion), kind=kCustom, calls=%fused_computation.1.clone | custom fusion | bytes 25166848 | tf_op jit(solution)/shard_map/jit(_take)/gather | solution.py:50
  101.3 14.6 %fusion = f32[256,128,128]{2,1,0:T(8,128)} fusion(bf16[256,192,128]{2,1,0:T(8,128)(2,1)} %gather_fusion.9, bf16[256,192,128]{2,1,0:T(8,128)(2,1)} %gather_fusion.8, pred[256]{0:T(512)(128)(4,1)S(1)} %get-tuple-element.7, pred[256]{0:T(512)(128)(4,1)S(1)} %get-tuple-element.8), kind=kOutput, calls=%fused_computation.10 | convolution fusion | flops 1623195648 | bytes 41943552 | tf_op jit(solution)/shard_map/rnc,rnd->ncd/dot_general | solution.py:52
  115.9 0.0 reduce-scatter.2.cloned.1.call-update
  115.9 0.0 all-gather.6.cloned.1.call-start
  116.0 183.9 %reduce-scatter.2.cloned.1.call-done = f32[16,128,128]{2,1,0:T(8,128)} async-done(((f32[256,128,128]{2,1,0:T(8,128)}), f32[16,128,128]{2,1,0:T(8,128)}) %reduce-scatter.2.cloned.1.call-update) | async-done | bytes 1048592 | tf_op jit(solution)/shard_map/reduce_scatter | solution.py:51
  299.9 3.2 sort.31
  303.1 2.2 gather_fusion.4
  305.3 0.1 reshape.98
  305.5 0.1 reshape.159
  305.6 12.9 %gather_fusion.5 = bf16[256,192,128]{2,1,0:T(8,128)(2,1)} fusion(bf16[192,64,128]{2,0,1:T(8,128)(2,1)} %copy-done.5, s32[1024]{0:T(1024)S(1)} %pad_clamp_fusion.3), kind=kCustom, calls=%fused_computation.7 | custom fusion | bytes 25166848 | tf_op jit(solution)/shard_map/gather | solution.py:35
  318.4 12.1 %gather_fusion = bf16[256,128,128]{2,1,0:T(8,128)(2,1)} fusion(bf16[256,128,128]{2,1,0:T(8,128)(2,1)} %all-gather.4.cloned.1.call-done, s32[1024]{0:T(1024)S(1)} %pad_clamp_fusion.6), kind=kCustom, calls=%fused_computation.2 | custom fusion | bytes 16778240 | tf_op jit(solution)/shard_map/gather | solution.py:34
  330.6 11.2 %fusion.18 = bf16[64,24,8,128]{3,2,1,0:T(8,128)(2,1)S(1)} fusion(bf16[64,4,128,128]{3,2,1,0:T(8,128)(2,1)} %bitcast.69, bf16[192,64,4,128]{3,0,2,1:T(8,128)(2,1)} %bitcast.68, bf16[192,8192]{1,0:T(8,128)(2,1)} %param.8), kind=kOutput, calls=%fused_computation.33 | convolution fusion | flops 1615331328 | bytes 27262976 | tf_op jit(solution)/shard_map/rnkd,nkcd->rnc/dot_general | solution.py:36
  341.8 2.5 copy.32
  344.3 161.1 %all-gather.6.cloned.1.call-done = f32[256,128,128]{2,1,0:T(8,128)} async-done(((f32[16,128,128]{2,1,0:T(8,128)}), f32[256,128,128]{2,1,0:T(8,128)}) %all-gather.6.cloned.1.call-update) | async-done | bytes 16777232 | tf_op jit(solution)/shard_map/all_gather | solution.py:57
  505.5 8.6 %reduce_sum.18 = f32[16,128,128]{2,1,0:T(8,128)} reduce(f32[16,16,128,128]{3,2,1,0:T(8,128)} %bitcast.66, f32[]{:T(128)} %constant.10.clone.1), dimensions={0}, to_apply=%region_3.5 | reduce | flops 3932160 | bytes 17825796 | tf_op jit(solution)/shard_map/reduce_sum | solution.py:57
  514.0 1.4 multiply_reduce_fusion
  515.5 2.3 broadcast_multiply_fusion
  (31 shorter events, 0.2 us)
Async XLA Ops:
  7.2 11.0 %copy-start = (bf16[192,8192]{1,0:T(8,128)(2,1)S(1)}, bf16[192,8192]{1,0:T(8,128)(2,1)}, u32[]{:S(2)}) copy-start(bf16[192,8192]{1,0:T(8,128)(2,1)} %param.7) | copy-start | bytes 9437188
  7.2 60.2 %all-gather.4.cloned.1.call-start = ((), (), s32[]{:S(2)}) async-start(), calls=%async_computation.1 | async-start | bytes 8912896 | tf_op jit(solution)/shard_map/all_gather | solution.py:29
  7.9 292.0 %reduce-scatter.2.cloned.1.call-start = ((), (), s32[]{:S(2)}) async-start(), calls=%async_computation.2 | async-start | bytes 17825792 | tf_op jit(solution)/shard_map/reduce_scatter | solution.py:51
  20.7 12.9 %copy-start.4 = (bf16[192,64,128]{2,0,1:T(8,128)(2,1)S(1)}, bf16[192,64,128]{2,0,1:T(8,128)(2,1)}, u32[]{:S(2)}) copy-start(bf16[192,64,128]{2,0,1:T(8,128)(2,1)} %copy_bitcast_fusion.1) | copy-start | bytes 9437188
  90.5 10.7 %copy-start.5 = (bf16[192,64,128]{2,0,1:T(8,128)(2,1)}, bf16[192,64,128]{2,0,1:T(8,128)(2,1)S(1)}, u32[]{:S(2)}) copy-start(bf16[192,64,128]{2,0,1:T(8,128)(2,1)S(1)} %fusion.13) | copy-start | bytes 9437188
  115.9 184.0 %copy-start.2 = (s32[256]{0:T(256)S(1)}, s32[256]{0:T(256)}, u32[]{:S(2)}) copy-start(s32[256]{0:T(256)} %param.11) | copy-start | bytes 3076
  115.9 187.2 %copy-start.3 = (s32[256]{0:T(256)S(1)}, s32[256]{0:T(256)}, u32[]{:S(2)}) copy-start(s32[256]{0:T(256)} %param.10) | copy-start | bytes 3076
  115.9 389.5 %all-gather.6.cloned.1.call-start = ((), (), s32[]{:S(2)}) async-start(), calls=%async_computation.3 | async-start | bytes 17825792 | tf_op jit(solution)/shard_map/all_gather | solution.py:57
  505.5 12.4 %copy-start.1 = (bf16[192,8192]{1,0:T(8,128)(2,1)S(1)}, bf16[192,8192]{1,0:T(8,128)(2,1)}, u32[]{:S(2)}) copy-start(bf16[192,8192]{1,0:T(8,128)(2,1)} %param.7) | copy-start | bytes 9437188
Sparse Core Ops, SparseCore 0:
  9.9 57.5 all-gather.3
  116.1 183.7 reduce-scatter.1
  302.3 203.1 all-gather.5
